TPU v7x, 32 devices: a whole 2x2x4 slice. The times are simulated.
32 devices in a mesh: dp: 8 (over y, x, core), seq: 4 (over z).
Axes of the slice: x: 2, y: 2, z: 4, core: 2. Of those that a mesh axis runs over, the one named last changes fastest.
Arguments:
- video: bfloat16 [8, 512, 3072], P('dp', 'seq'), may hold values from -6 to 6
- cotangent: bfloat16 [8, 512, 3072], P('dp', 'seq'), may hold values from -6 to 6
- w_query: bfloat16 [3072, 3072], P(None, 'seq'), may hold values from -0.109375 to 0.109375
- w_out: bfloat16 [3072, 3072], P('seq'), may hold values from -0.109375 to 0.109375
- ref_kv: bfloat16 [8, 2, 1024, 3072], P('dp', None, 'seq'), may hold values from -400 to 400, as said below
- tile_lists: int32 [8, 2, 4, 3], P('dp'), may hold values from -1 to 3, as said below
Outputs:
- output: bfloat16 [8, 512, 3072], P('dp', 'seq')
- grad_video: bfloat16 [8, 512, 3072], P('dp', 'seq')
- grad_wq: float32 [3072, 3072], P(None, 'seq')
- grad_wo: float32 [3072, 3072], P('seq')
- grad_ref: bfloat16 [8, 2, 1024, 3072], P('dp', None, 'seq')
Inputs may be any that keep to these rules, and one draw needn't show every extreme that they name: `ref_kv`: values are of order one; key rows may carry scales of up to some tens. `tile_lists`: each row lists first 1 to 3 different tile indices from 0 to 3, consecutive modulo 4, then -1; the first video tile of every clip lists exactly 3 tiles for each person.
All inputs are finite; a program needn't handle non-finite values.
Results may differ from a plain program's by a relative error of at most 0.012.
The roundings to bfloat16 on the way count: a program that leaves them out, or rounds other values in their place, can miss the bound.
Values may be sent and summed in bfloat16 or wider, within the bound.
No kernel may reach another device: no remote copies, remote signals or barrier semaphores. Data moves between devices by JAX's collectives and lax.ppermute only.
A program may use at most 128 MiB of HBM per device.

v0:
```python
import math
import jax
import jax.numpy as jnp
from jax import lax
from jax.sharding import PartitionSpec as P

HD = 128
REF = 512
TILE = 128


def build_allowed(tile_lists, tile_size, ref_tokens):
    tiles_each = ref_tokens // tile_size
    matched = jnp.any(tile_lists[..., None] == jnp.arange(tiles_each, dtype=jnp.int32), axis=-2)
    tile_table = jnp.transpose(matched, (1, 0, 2)).reshape(matched.shape[1], -1)
    return jnp.repeat(jnp.repeat(tile_table, tile_size, axis=0), tile_size, axis=1)


def split_heads(array, heads_count):
    return jnp.transpose(array.reshape(array.shape[0], heads_count, -1), (1, 0, 2))


def merge_heads(array):
    return jnp.transpose(array, (1, 0, 2)).reshape(array.shape[1], -1)


def contract_last(left, right):
    return lax.dot_general(
        left, right, (((1,), (1,)), ((), ())), preferred_element_type=jnp.float32
    )


def contract_first(left, right):
    return lax.dot_general(
        left, right, (((0,), (0,)), ((), ())), preferred_element_type=jnp.float32
    )


def softmax_weights(query, keys, allowed, score_scale):
    scores = contract_last(query, keys) * score_scale
    scores = jnp.where(allowed, scores, -1e30)
    peak = jnp.max(scores, axis=-1, keepdims=True)
    weights = jnp.exp(scores - peak)
    return weights / jnp.sum(weights, axis=-1, keepdims=True)


def head_forward(query, keys, values, allowed, score_scale):
    weights = softmax_weights(query, keys, allowed, score_scale)
    probs = weights.astype(jnp.bfloat16)
    return jnp.dot(probs, values, preferred_element_type=jnp.float32).astype(jnp.bfloat16)


def head_backward(query, keys, values, grad_out, allowed, score_scale):
    weights = softmax_weights(query, keys, allowed, score_scale)
    probs = weights.astype(jnp.bfloat16)
    grad_probs = contract_last(grad_out, values)
    delta = jnp.sum(grad_probs * weights, axis=-1, keepdims=True)
    grad_scores = (weights * (grad_probs - delta) * score_scale).astype(jnp.bfloat16)
    grad_query = jnp.dot(grad_scores, keys, preferred_element_type=jnp.float32).astype(jnp.bfloat16)
    grad_keys = contract_first(grad_scores, query).astype(jnp.bfloat16)
    grad_values = contract_first(probs, grad_out).astype(jnp.bfloat16)
    return (grad_query, grad_keys, grad_values)


def body(video, cotangent, w_query, w_out, ref_kv, tile_lists):
    local_width = w_query.shape[1]
    heads_here = local_width // HD
    score_scale = 1.0 / math.sqrt(HD)
    gathered = lax.all_gather(video, "seq", axis=1, tiled=True)[0]
    query = jnp.dot(gathered, w_query, preferred_element_type=jnp.float32).astype(jnp.bfloat16)
    both_kv = lax.all_to_all(ref_kv, "seq", split_axis=3, concat_axis=2, tiled=True)[0]
    allowed = build_allowed(tile_lists[0], TILE, REF)
    q_heads = split_heads(query, heads_here)
    k_heads = split_heads(both_kv[0], heads_here)
    v_heads = split_heads(both_kv[1], heads_here)
    attn_heads = lax.map(
        lambda item: head_forward(item[0], item[1], item[2], allowed, score_scale),
        (q_heads, k_heads, v_heads),
    )
    attention = merge_heads(attn_heads)
    rows = attention
    output = lax.psum_scatter(
        jnp.dot(rows, w_out, preferred_element_type=jnp.float32),
        "seq",
        scatter_dimension=0,
        tiled=True,
    )
    output = output.astype(jnp.bfloat16)[None]
    grad_rows = lax.all_gather(cotangent, "seq", axis=1, tiled=True)[0]
    grad_attention = contract_last(grad_rows, w_out).astype(jnp.bfloat16)
    grad_wo = contract_first(attention, grad_rows)
    back = lax.map(
        lambda item: head_backward(item[0], item[1], item[2], item[3], allowed, score_scale),
        (q_heads, k_heads, v_heads, split_heads(grad_attention, heads_here)),
    )
    grad_query = merge_heads(back[0])
    grad_kv = jnp.stack([merge_heads(back[1]), merge_heads(back[2])])[None]
    grad_ref = lax.all_to_all(grad_kv, "seq", split_axis=2, concat_axis=3, tiled=True)
    rows = grad_query
    grad_video = lax.psum_scatter(
        contract_last(rows, w_query).astype(jnp.bfloat16), "seq", scatter_dimension=0, tiled=True
    ).astype(jnp.float32)
    grad_video = grad_video.astype(jnp.bfloat16)[None]
    grad_wq = contract_first(gathered, grad_query)
    grad_wq, grad_wo = (
        lax.psum(grad_wq.astype(jnp.bfloat16), "dp").astype(jnp.float32),
        lax.psum(grad_wo.astype(jnp.bfloat16), "dp").astype(jnp.float32),
    )
    return (output, grad_video, grad_wq, grad_wo, grad_ref)


def solution(mesh):
    in_specs = (
        P("dp", "seq", None),
        P("dp", "seq", None),
        P(None, "seq"),
        P("seq", None),
        P("dp", None, "seq", None),
        P("dp", None, None, None),
    )
    out_specs = (
        P("dp", "seq", None),
        P("dp", "seq", None),
        P(None, "seq"),
        P("seq", None),
        P("dp", None, "seq", None),
    )
    return jax.shard_map(body, mesh=mesh, in_specs=in_specs, out_specs=out_specs, check_vma=False)
```

profile of v0, /device:TPU:0, one launch (start us, length us, event | category | flops | bytes accessed | tf_op | source)
XLA Modules:
  0.0 661.5 jit_solution(8851351125706962845)
XLA Ops:
  8.6 8.6 %copy.77 = bf16[1,2,256,3072]{2,1,0,3:T(2,128)(2,1)} copy(bf16[1,2,256,3072]{3,2,1,0:T(8,128)(2,1)} %param.14) | data formatting | bytes 6291456 | tf_op args[4]
  17.3 6.4 all-to-all-start
  24.1 109.5 %all-gather.5.cloned.1.call-done = bf16[1,512,3072]{2,1,0:T(8,128)(2,1)} async-done(((bf16[1,128,3072]{2,1,0:T(8,128)(2,1)}), bf16[1,512,3072]{2,1,0:T(8,128)(2,1)}) %all-gather.5.cloned.1.call-update) | async-done | bytes 3145744 | tf_op jit(solution)/shard_map/all_gather | solution.py:89
  133.5 6.8 %fusion.51 = bf16[512,768]{1,0:T(8,128)(2,1)} fusion(bf16[768,3072]{1,0:T(8,128)(2,1)} %param.13, bf16[1,512,3072]{2,1,0:T(8,128)(2,1)} %all-gather.5.cloned.1.call-done), kind=kOutput, calls=%fused_computation.66 | convolution fusion | flops 2416312320 | bytes 8650752 | tf_op jit(solution)/shard_map/dot_general | solution.py:28
  140.4 2.4 copy.86
  142.7 54.0 %all-gather.3.cloned.1.call-done = bf16[1,512,3072]{2,1,0:T(8,128)(2,1)} async-done(((bf16[1,128,3072]{2,1,0:T(8,128)(2,1)}), bf16[1,512,3072]{2,1,0:T(8,128)(2,1)}) %all-gather.3.cloned.1.call-update) | async-done | bytes 3145744 | tf_op jit(solution)/shard_map/all_gather | solution.py:69
  196.7 6.8 %fusion.48 = bf16[512,768]{1,0:T(8,128)(2,1)} fusion(bf16[3072,768]{1,0:T(8,128)(2,1)} %param.12, bf16[1,512,3072]{2,1,0:T(8,128)(2,1)} %all-gather.3.cloned.1.call-done), kind=kOutput, calls=%fused_computation.65 | convolution fusion | flops 2416312320 | bytes 8650752 | tf_op jit(solution)/shard_map/dot_general | solution.py:70
  203.5 2.3 copy.76
  205.8 2.3 copy.82
  208.1 2.4 copy.113
  210.5 2.2 fusion.57
  212.7 2.8 reshape_squeeze.7
  219.9 32.9 %while.26 = (s32[]{:T(128)}, bf16[6,512,128]{1,2,0:T(8,128)(2,1)S(1)}, bf16[6,512,128]{2,1,0:T(8,128)(2,1)}, bf16[6,1024,128]{2,1,0:T(8,128)(2,1)}, bf16[6,1024,...) while((s32[]{:T(128)}, bf16[6,512,128]{1,2,0:T(8,128)(2,1)S(1)}, ...), condition=%wide.region_4.5_spmd.clone, body=%wide.region_1.4_spmd.clone.sunk | while | flops 272694272 | bytes 8666205 | solution.py:76
  253.8 76.0 %while.27 = (s32[]{:T(128)}, bf16[6,512,128]{1,2,0:T(8,128)(2,1)}, bf16[6,1024,128]{1,2,0:T(8,128)(2,1)}, bf16[6,1024,128]{1,2,0:T(8,128)(2,1)}, bf16[6,512,128]...) while((s32[]{:T(128)}, bf16[6,512,128]{1,2,0:T(8,128)(2,1)}, ...), condition=%wide.region_10.11_spmd.clone, body=%wide.region_6.10_spmd.clone.sunk | while | flops 680851968 | bytes 23490688 | solution.py:92
  259.3 1.8 multiply_reduce_fusion.2
  272.0 1.8 multiply_reduce_fusion.2
  284.7 1.8 multiply_reduce_fusion.2
  329.8 7.1 %fusion.41 = bf16[3072,768]{0,1:T(8,128)(2,1)} fusion(bf16[512,768]{0,1:T(8,128)(2,1)} %bitcast.173, bf16[1,512,3072]{2,1,0:T(8,128)(2,1)} %all-gather.3.cloned.1.call-done), kind=kOutput, calls=%fused_computation.55 | convolution fusion | flops 2418278400 | bytes 8650752 | tf_op jit(solution)/shard_map/dot_general | solution.py:34
  336.9 4.2 convolution_convert_fusion.4
  341.2 7.1 %fusion.58 = f32[512,3072]{1,0:T(8,128)} fusion(bf16[512,768]{0,1:T(8,128)(2,1)S(1)} %bitcast.168, bf16[768,3072]{1,0:T(8,128)(2,1)} %param.13), kind=kOutput, calls=%fused_computation.73 | convolution fusion | flops 2415919104 | bytes 11796480 | tf_op jit(solution)/shard_map/dot_general | solution.py:83
  349.4 6.5 convolution_convert_fusion.6
  356.0 2.3 maximum_bitcast_fusion
  358.3 5.6 copy.94
  363.9 74.7 %all_to_all.33 = bf16[1,2,1024,768]{3,1,0,2:T(2,128)(2,1)S(1)} all-to-all(bf16[1,2,1024,768]{3,1,0,2:T(2,128)(2,1)} %copy.94), channel_id=1, replica_groups=mesh['dp'=8,'seq'=4] {'seq'}, dimensions={2} | all-to-all | bytes 6291456 | tf_op jit(solution)/shard_map/all_to_all | solution.py:98
  439.1 2.8 copy.96
  441.9 4.7 copy.98
  446.6 31.6 %all-reduce.3.cloned.1.call-done = (bf16[3072,768]{0,1:T(8,128)(2,1)}, bf16[768,3072]{1,0:T(8,128)(2,1)}) async-done(((bf16[3072,768]{0,1:T(8,128)(2,1)}, bf16[768,3072]{1,0:T(8,128)(2,1)}), (bf16[3072,768]{0,1:T(8,128)(2,1)}, bf16[768,3072]{1,0:T(8,128)(2,1)})) %all-reduce.3.cloned.1.call-update) | async-done | bytes 9437200 | tf_op jit(solution)/shard_map/psum | solution.py:106
  478.2 7.4 %copy.97 = f32[3072,768]{1,0:T(8,128)} copy(bf16[3072,768]{0,1:T(8,128)(2,1)} %get-tuple-element.241) | data formatting | bytes 14155776
  485.6 8.5 %convert_element_type.58 = f32[768,3072]{1,0:T(8,128)} convert(bf16[768,3072]{1,0:T(8,128)(2,1)} %get-tuple-element.242) | non-fusion elementwise | flops 2359296 | bytes 14155776 | tf_op jit(solution)/shard_map/convert_element_type | solution.py:107
  494.1 97.3 %reduce-scatter.3.cloned.1.call-done = f32[128,3072]{1,0:T(8,128)} async-done(((f32[512,3072]{1,0:T(8,128)}), f32[128,3072]{1,0:T(8,128)}) %reduce-scatter.3.cloned.1.call-update) | async-done | bytes 1572880 | tf_op jit(solution)/shard_map/reduce_scatter | solution.py:82
  591.3 2.4 convert_bitcast_fusion
  593.7 61.3 %reduce-scatter.5.cloned.1.call-done = bf16[128,3072]{1,0:T(8,128)(2,1)} async-done(((bf16[512,3072]{1,0:T(8,128)(2,1)}), bf16[128,3072]{1,0:T(8,128)(2,1)}) %reduce-scatter.5.cloned.1.call-update) | async-done | bytes 786448 | tf_op jit(solution)/shard_map/reduce_scatter | solution.py:100
  (141 shorter events, 111.4 us)
Async XLA Ops:
  7.2 126.4 %all-gather.5.cloned.1.call-start = ((), (), s32[]{:S(2)}) async-start(), calls=%async_computation.6 | async-start | bytes 3932160 | tf_op jit(solution)/shard_map/all_gather | solution.py:89
  7.9 188.8 %all-gather.3.cloned.1.call-start = ((), (), s32[]{:S(2)}) async-start(), calls=%async_computation.4 | async-start | bytes 3932160 | tf_op jit(solution)/shard_map/all_gather | solution.py:69
  17.3 6.5 copy-start.1
  17.3 190.8 %all-to-all-start = ((bf16[1,2,256,3072]{2,1,0,3:T(2,128)(2,1)}), bf16[1,2,256,3072]{2,1,0,3:T(2,128)(2,1)S(1)}, u32[]{:S(2)}, u32[]{:S(2)}) async-start(bf16[1,2,256,3072]{2,1,0,3:T(2,128)(2,1)} %copy.77), calls=%async_computation | async-start | bytes 6291456 | tf_op jit(solution)/shard_map/all_to_all | solution.py:71
  23.7 454.5 %all-reduce.3.cloned.1.call-start = ((), (), s32[]{:S(2)}) async-start(), calls=%async_computation.8 | async-start | bytes 18874368 | tf_op jit(solution)/shard_map/psum | solution.py:106
  329.8 7.1 %copy-start.2 = (bf16[1,512,3072]{2,1,0:T(8,128)(2,1)S(1)}, bf16[1,512,3072]{2,1,0:T(8,128)(2,1)}, u32[]{:S(2)}) copy-start(bf16[1,512,3072]{2,1,0:T(8,128)(2,1)} %all-gather.5.cloned.1.call-done) | copy-start | bytes 9437188
  341.1 250.2 %reduce-scatter.3.cloned.1.call-start = ((), (), s32[]{:S(2)}) async-start(), calls=%async_computation.5 | async-start | bytes 7864320 | tf_op jit(solution)/shard_map/reduce_scatter | solution.py:82
  348.3 1.1 copy-start
  348.3 306.6 %reduce-scatter.5.cloned.1.call-start = ((), (), s32[]{:S(2)}) async-start(), calls=%async_computation.7 | async-start | bytes 3932160 | tf_op jit(solution)/shard_map/reduce_scatter | solution.py:100
Sparse Core Ops, SparseCore 0:
  9.6 123.9 all-gather.4
  135.1 61.5 all-gather.2
  341.3 136.9 all-reduce.2
  480.5 110.8 reduce-scatter.2
  594.2 60.7 reduce-scatter.4
where the time goes:
time: 664 us; the launch traced here: 662 us
  waiting for transfers between devices  355 us (53%)
  matrix products  106 us (16%)
  local copies, waits for them, and re-layouts  82 us (12%)
  blocking collectives  74.7 us (11%)
  other arithmetic  23.1 us (3%)
  between operations  13.8 us (2%)
    all_gather x1, waiting for transfers between devices, body(): grad_rows = lax.all_gather(cotangent, 'seq', axis=1, tiled=True)[0]  109 us
    reduce_scatter x1, waiting for transfers between devices, body(): lax.psum_scatter(jnp.dot(rows, w_out, preferred_element_type=jnp.float32)...  97.3 us
    all_to_all x1, blocking collectives, body(): lax.all_to_all(grad_kv, 'seq', split_axis=2, concat_axis=3, tiled=True)  74.7 us
    reduce_scatter x1, waiting for transfers between devices, body(): lax.psum_scatter(contract_last(rows, w_query).astype(jnp.bfloat16), 'seq'...  61.3 us
    all_gather x1, waiting for transfers between devices, body(): gathered = lax.all_gather(video, 'seq', axis=1, tiled=True)[0]  54 us
    dot_general x20, matrix products, contract_last(): lax.dot_general(left, right, (((1,), (1,)), ((), ())), preferred_element_...  44.7 us
    psum x1, waiting for transfers between devices, body(): lax.psum(grad_wq.astype(jnp.bfloat16), 'dp').astype(jnp.float32)  31.6 us
    dot_general x14, matrix products, contract_first(): lax.dot_general(left, right, (((0,), (0,)), ((), ())), preferred_element_...  29.6 us
  transfers between devices with their start and end apart: 6, of which 5 were waited for; matrix products, arithmetic and copies ran while one was open for 12% of the time, Pallas kernels for 0%

commit v1 on v0

--- a/solution.py
+++ b/solution.py
@@ -7,6 +7,27 @@
 HD = 128
 REF = 512
 TILE = 128
+
+
+def joined_along(parts, dim):
+    shape = list(parts.shape[1:])
+    shape[dim] *= parts.shape[0]
+    return jnp.moveaxis(parts, 0, dim).reshape(shape)
+
+
+def collected_by_bits(array, axis):
+    length, position = (lax.axis_size(axis), lax.axis_index(axis))
+    pieces, bit = (array[None], 1)
+    while bit < length:
+        other = lax.ppermute(pieces, axis, [(i, i ^ bit) for i in range(length)])
+        low = position & bit == 0
+        pieces = jnp.concatenate([jnp.where(low, pieces, other), jnp.where(low, other, pieces)])
+        bit *= 2
+    return pieces
+
+
+def collect(array, axis, dim):
+    return joined_along(collected_by_bits(array, axis), dim)
 
 
 def build_allowed(tile_lists, tile_size, ref_tokens):
@@ -86,7 +107,7 @@
         tiled=True,
     )
     output = output.astype(jnp.bfloat16)[None]
-    grad_rows = lax.all_gather(cotangent, "seq", axis=1, tiled=True)[0]
+    grad_rows = collect(cotangent, "seq", 1)[0]
     grad_attention = contract_last(grad_rows, w_out).astype(jnp.bfloat16)
     grad_wo = contract_first(attention, grad_rows)
     back = lax.map(

time: 664 us -> 689 us (1.038)
  waiting for transfers between devices: 355 us -> 372 us
    ppermute x0 -> x2, waiting for transfers between devices: none -> 181 us  [collected_by_bits(): other = lax.ppermute(pieces, axis, [(i, i ^ bit) for i in range(length)])]
    all_gather x1 -> x0, waiting for transfers between devices: 109 us -> none  [body(): grad_rows = lax.all_gather(cotangent, 'seq', axis=1, tiled=True)[0]]
    all_gather x1, waiting for transfers between devices: 54 us -> 0.01 us  [body(): gathered = lax.all_gather(video, 'seq', axis=1, tiled=True)[0]]
    unnamed x12 -> x22, local copies, waits for them, and re-layouts: 27.2 us -> 29 us
  transfers between devices with their start and end apart: 6 -> 7, of which waited for: 5 -> 5; matrix products, arithmetic and copies ran while one was open for 12% -> 12% of each run, Pallas kernels for 0% -> 0%
where the time goes in v1:
time: 689 us; the launch traced here: 687 us
  waiting for transfers between devices  372 us (54%)
  matrix products  104 us (15%)
  local copies, waits for them, and re-layouts  83.8 us (12%)
  blocking collectives  74.7 us (11%)
  other arithmetic  28.2 us (4%)
  between operations  13.9 us (2%)
  starting transfers between devices  8.87 us (1%)
    ppermute x2, waiting for transfers between devices, collected_by_bits(): other = lax.ppermute(pieces, axis, [(i, i ^ bit) for i in range(length)])  181 us
    reduce_scatter x1, waiting for transfers between devices, body(): lax.psum_scatter(jnp.dot(rows, w_out, preferred_element_type=jnp.float32)...  97.4 us
    all_to_all x1, blocking collectives, body(): lax.all_to_all(grad_kv, 'seq', split_axis=2, concat_axis=3, tiled=True)  74.7 us
    reduce_scatter x1, waiting for transfers between devices, body(): lax.psum_scatter(contract_last(rows, w_query).astype(jnp.bfloat16), 'seq'...  61.3 us
    dot_general x20, matrix products, contract_last(): lax.dot_general(left, right, (((1,), (1,)), ((), ())), preferred_element_...  43.1 us
    psum x1, waiting for transfers between devices, body(): lax.psum(grad_wq.astype(jnp.bfloat16), 'dp').astype(jnp.float32)  32.3 us
    dot_general x14, matrix products, contract_first(): lax.dot_general(left, right, (((0,), (0,)), ((), ())), preferred_element_...  30.3 us
    unnamed x22, local copies, waits for them, and re-layouts  29 us
  transfers between devices with their start and end apart: 7, of which 5 were waited for; matrix products, arithmetic and copies ran while one was open for 12% of the time, Pallas kernels for 0%

profile of v1, /device:TPU:0, one launch (start us, length us, event | category | flops | bytes accessed | tf_op | source)
XLA Modules:
  0.0 686.8 jit_solution(709470550394449186)
XLA Ops:
  7.2 3.1 collective-permute-start
  10.3 8.6 %copy.77 = bf16[1,2,256,3072]{2,1,0,3:T(2,128)(2,1)} copy(bf16[1,2,256,3072]{3,2,1,0:T(8,128)(2,1)} %param.14) | data formatting | bytes 6291456 | tf_op args[4]
  19.0 3.9 all-to-all-start
  22.9 22.4 %collective-permute-done = bf16[1,1,128,3072]{3,2,1,0:T(8,128)(2,1)} collective-permute-done((bf16[1,1,128,3072]{3,2,1,0:T(8,128)(2,1)}, bf16[1,1,128,3072]{3,2,1,0:T(8,128)(2,1)}, u32[]{:S(2)}, u32[]{:S(2)}) %collective-permute-start) | collective-permute-done | bytes 786464 | tf_op jit(solution)/shard_map/ppermute | solution.py:22
  51.0 158.9 %collective-permute-done.1 = bf16[2,1,128,3072]{3,2,1,0:T(8,128)(2,1)} collective-permute-done((bf16[2,1,128,3072]{3,2,1,0:T(8,128)(2,1)}, bf16[2,1,128,3072]{3,2,1,0:T(8,128)(2,1)}, u32[]{:S(2)}, u32[]{:S(2)}) %collective-permute-start.1) | collective-permute-done | bytes 1572896 | tf_op jit(solution)/shard_map/ppermute | solution.py:22
  209.9 2.0 broadcast_select_fusion.1
  213.9 5.9 convolution_convert_fusion.7
  219.8 2.3 copy.86
  222.1 6.8 fusion.45
  228.9 2.3 copy.76
  231.2 2.3 copy.82
  233.4 2.4 copy.113
  235.9 2.2 fusion.51
  238.1 2.8 reshape_squeeze.7
  244.6 32.2 %while.26 = (s32[]{:T(128)}, bf16[6,512,128]{1,2,0:T(8,128)(2,1)S(1)}, bf16[6,512,128]{2,1,0:T(8,128)(2,1)}, bf16[6,1024,128]{2,1,0:T(8,128)(2,1)S(1)}, bf16[6,1...) while((s32[]{:T(128)}, bf16[6,512,128]{1,2,0:T(8,128)(2,1)S(1)}, ...), condition=%wide.region_4.5_spmd.clone, body=%wide.region_1.4_spmd.clone.sunk | while | flops 272694272 | bytes 8666205 | solution.py:97
  278.0 76.8 %while.27 = (s32[]{:T(128)}, bf16[6,512,128]{1,2,0:T(8,128)(2,1)}, bf16[6,1024,128]{1,2,0:T(8,128)(2,1)}, bf16[6,1024,128]{1,2,0:T(8,128)(2,1)}, bf16[6,512,128]...) while((s32[]{:T(128)}, bf16[6,512,128]{1,2,0:T(8,128)(2,1)}, ...), condition=%wide.region_10.11_spmd.clone, body=%wide.region_6.10_spmd.clone.sunk | while | flops 680851968 | bytes 36073656 | solution.py:113
  334.7 1.8 multiply_reduce_fusion.2
  354.8 7.1 %convolution_convert_fusion.4 = bf16[768,3072]{1,0:T(8,128)(2,1)} fusion(bf16[512,768]{0,1:T(8,128)(2,1)} %bitcast.168, bf16[512,3072]{1,0:T(8,128)(2,1)} %bitcast.167), kind=kOutput, calls=%fused_computation.53 | convolution fusion | flops 2418278400 | bytes 8650752 | tf_op jit(solution)/shard_map/dot_general | solution.py:55
  361.8 4.2 fusion.41
  367.2 6.9 %fusion.52 = f32[512,3072]{1,0:T(8,128)} fusion(bf16[512,768]{0,1:T(8,128)(2,1)S(1)} %bitcast.169, bf16[768,3072]{1,0:T(8,128)(2,1)} %param.13), kind=kOutput, calls=%fused_computation.76 | convolution fusion | flops 2415919104 | bytes 11796480 | tf_op jit(solution)/shard_map/dot_general | solution.py:104
  374.2 6.5 convolution_convert_fusion.6
  380.7 2.2 maximum_bitcast_fusion
  382.9 5.6 copy.94
  388.6 74.7 %all_to_all.33 = bf16[1,2,1024,768]{3,1,0,2:T(2,128)(2,1)S(1)} all-to-all(bf16[1,2,1024,768]{3,1,0,2:T(2,128)(2,1)} %copy.94), channel_id=1, replica_groups=mesh['dp'=8,'seq'=4] {'seq'}, dimensions={2} | all-to-all | bytes 6291456 | tf_op jit(solution)/shard_map/all_to_all | solution.py:119
  463.7 2.8 copy.96
  466.5 4.6 copy.98
  471.1 32.3 %all-reduce.3.cloned.1.call-done = (bf16[3072,768]{0,1:T(8,128)(2,1)}, bf16[768,3072]{1,0:T(8,128)(2,1)}) async-done(((bf16[3072,768]{0,1:T(8,128)(2,1)}, bf16[768,3072]{1,0:T(8,128)(2,1)}), (bf16[3072,768]{0,1:T(8,128)(2,1)}, bf16[768,3072]{1,0:T(8,128)(2,1)})) %all-reduce.3.cloned.1.call-update) | async-done | bytes 9437200 | tf_op jit(solution)/shard_map/psum | solution.py:127
  503.4 7.4 %copy.97 = f32[3072,768]{1,0:T(8,128)} copy(bf16[3072,768]{0,1:T(8,128)(2,1)} %get-tuple-element.241) | data formatting | bytes 14155776
  510.8 8.5 %convert_element_type.58 = f32[768,3072]{1,0:T(8,128)} convert(bf16[768,3072]{1,0:T(8,128)(2,1)} %get-tuple-element.242) | non-fusion elementwise | flops 2359296 | bytes 14155776 | tf_op jit(solution)/shard_map/convert_element_type | solution.py:128
  519.3 97.4 %reduce-scatter.3.cloned.1.call-done = f32[128,3072]{1,0:T(8,128)} async-done(((f32[512,3072]{1,0:T(8,128)}), f32[128,3072]{1,0:T(8,128)}) %reduce-scatter.3.cloned.1.call-update) | async-done | bytes 1572880 | tf_op jit(solution)/shard_map/reduce_scatter | solution.py:103
  616.6 2.4 convert_bitcast_fusion
  619.0 61.3 %reduce-scatter.5.cloned.1.call-done = bf16[128,3072]{1,0:T(8,128)(2,1)} async-done(((bf16[512,3072]{1,0:T(8,128)(2,1)}), bf16[128,3072]{1,0:T(8,128)(2,1)}) %reduce-scatter.5.cloned.1.call-update) | async-done | bytes 786448 | tf_op jit(solution)/shard_map/reduce_scatter | solution.py:121
  (180 shorter events, 120.5 us)
Async XLA Ops:
  7.2 214.9 %all-gather.2.cloned.1.call-start = ((), (), s32[]{:S(2)}) async-start(), calls=%async_computation.4 | async-start | bytes 3932160 | tf_op jit(solution)/shard_map/all_gather | solution.py:90
  7.2 38.0 %collective-permute-start = (bf16[1,1,128,3072]{3,2,1,0:T(8,128)(2,1)}, bf16[1,1,128,3072]{3,2,1,0:T(8,128)(2,1)}, u32[]{:S(2)}, u32[]{:S(2)}) collective-permute-start(bf16[1,1,128,3072]{3,2,1,0:T(8,128)(2,1)} %bitcast.176), channel_id=1, source_target_pairs={{0,1},{1,0},{2,3},{3,2},{4,5},{5,4},{6,7},{7,6},{8,9},{9,8},{10,11... | collective-permute-start | bytes 2359304 | tf_op jit(solution)/shard_map/ppermute | solution.py:22
  19.0 214.5 %all-to-all-start = ((bf16[1,2,256,3072]{2,1,0,3:T(2,128)(2,1)}), bf16[1,2,256,3072]{2,1,0,3:T(2,128)(2,1)S(1)}, u32[]{:S(2)}, u32[]{:S(2)}) async-start(bf16[1,2,256,3072]{2,1,0,3:T(2,128)(2,1)} %copy.77), calls=%async_computation | async-start | bytes 6291456 | tf_op jit(solution)/shard_map/all_to_all | solution.py:92
  22.8 480.5 %all-reduce.3.cloned.1.call-start = ((), (), s32[]{:S(2)}) async-start(), calls=%async_computation.7 | async-start | bytes 18874368 | tf_op jit(solution)/shard_map/psum | solution.py:127
  46.7 0.9 copy-start
  46.7 2.2 copy-start.1
  46.7 3.9 copy-start.8
  48.9 161.0 %collective-permute-start.1 = (bf16[2,1,128,3072]{3,2,1,0:T(8,128)(2,1)}, bf16[2,1,128,3072]{3,2,1,0:T(8,128)(2,1)}, u32[]{:S(2)}, u32[]{:S(2)}) collective-permute-start(bf16[2,1,128,3072]{3,2,1,0:T(8,128)(2,1)} %pad_maximum_fusion.1), channel_id=1, source_target_pairs={{0,2},{1,3},{2,0},{3,1},{4,6},{5,7},{6,4},{7,5},{8,10},{9,11},{10,... | collective-permute-start | bytes 4718600 | tf_op jit(solution)/shard_map/ppermute | solution.py:22
  212.2 1.7 copy-start.4
  276.8 1.1 copy-start.5
  278.0 1.6 copy-start.2
  287.5 3.3 copy-start.3
  290.8 1.6 copy-start.2
  300.3 3.3 copy-start.3
  303.5 1.6 copy-start.2
  313.0 3.3 copy-start.3
  316.3 1.6 copy-start.2
  325.8 3.3 copy-start.3
  329.2 1.6 copy-start.2
  338.6 3.3 copy-start.3
  342.0 1.6 copy-start.2
  351.5 3.3 copy-start.3
  354.8 7.1 %copy-start.7 = (bf16[6,512,128]{1,2,0:T(8,128)(2,1)S(1)}, bf16[6,512,128]{1,2,0:T(8,128)(2,1)}, u32[]{:S(2)}) copy-start(bf16[6,512,128]{1,2,0:T(8,128)(2,1)} %get-tuple-element.87) | copy-start | bytes 2359300
  354.8 7.1 %copy-start.9 = (bf16[1,512,3072]{2,1,0:T(8,128)(2,1)S(1)}, bf16[1,512,3072]{2,1,0:T(8,128)(2,1)}, u32[]{:S(2)}) copy-start(bf16[1,512,3072]{2,1,0:T(8,128)(2,1)} %all-gather.2.cloned.1.call-done) | copy-start | bytes 9437188
  366.1 1.1 copy-start.6
  366.1 250.5 %reduce-scatter.3.cloned.1.call-start = ((), (), s32[]{:S(2)}) async-start(), calls=%async_computation.5 | async-start | bytes 7864320 | tf_op jit(solution)/shard_map/reduce_scatter | solution.py:103
  374.1 306.2 %reduce-scatter.5.cloned.1.call-start = ((), (), s32[]{:S(2)}) async-start(), calls=%async_computation.6 | async-start | bytes 3932160 | tf_op jit(solution)/shard_map/reduce_scatter | solution.py:121
Sparse Core Ops, SparseCore 0:
  10.4 156.3 all-gather.1
  366.2 137.0 all-reduce.2
  505.8 110.8 reduce-scatter.2
  619.5 60.7 reduce-scatter.4
